TPU v7x, 256 devices: a whole 4x4x8 slice. The times are simulated.
256 devices in a mesh: seq: 64 (over y, z, x_lo), head: 4 (over x_hi, core).
Axes of the slice: x: 4 (x_hi: 2, x_lo: 2; x = x_hi * 2 + x_lo), y: 4, z: 8, core: 2. Of those that a mesh axis runs over, the one named last changes fastest.
Arguments:
- inputs: bfloat16 [32768, 5376], P('seq'), may hold values from -6 to 6
- queries: bfloat16 [32768, 16, 128], P('seq', 'head'), may hold values from -24 to 24
- out_grad: bfloat16 [32768, 16, 128], P('seq', 'head'), may hold values from -6 to 6
- segment_ids: int32 [32768], P('seq'), may hold values from 0 to 63, never falling along the last dimension, each value on 1 to 2048 neighbouring positions
- k_weight: bfloat16 [5376, 1024], P('seq', 'head'), may hold values from -0.078125 to 0.078125
- v_weight: bfloat16 [5376, 1024], P('seq', 'head'), may hold values from -0.078125 to 0.078125
- k_gain: float32 [128], replicated, may hold values from 0.1 to 1.9
Outputs:
- inputs_grad: bfloat16 [32768, 5376], P('seq', 'head')
- query_grad: bfloat16 [32768, 16, 128], P('seq', 'head')
- k_weight_grad: float32 [5376, 1024], P('seq', 'head')
- v_weight_grad: float32 [5376, 1024], P('seq', 'head')
Inputs may be any that keep to these rules, and one draw needn't show every extreme that they name: `segment_ids`: tokens of one packed document share an id; ids never fall along the row; a document holds at most 2048 tokens.
All inputs are finite; a program needn't handle non-finite values.
Results may differ from a plain program's by a relative error of at most 0.01065.
The roundings to bfloat16 on the way count: a program that leaves them out, or rounds other values in their place, can miss the bound.
Values may be sent and summed in bfloat16 or wider, within the bound.
No kernel may reach another device: no remote copies, remote signals or barrier semaphores. Data moves between devices by JAX's collectives and lax.ppermute only.
A program may use at most 128 MiB of HBM per device.

v0:
```python
import jax
import jax.numpy as jnp
from jax import lax
from jax.sharding import PartitionSpec as P

WIN = 1024
TOK_DEV = 512
score_scale = 168.0 ** (-0.5)


def shifted(block, axis, distance):
    devices = range(lax.axis_size(axis))
    route = [(i - distance, i) for i in devices if i - distance in devices]
    return lax.ppermute(block, axis, route)


def make_allowed(query_pos, query_seg, key_pos, key_seg):
    distance = query_pos[:, None] - key_pos[None, :]
    return (
        (distance >= 0)
        & (distance < WIN)
        & (query_seg[:, None] == key_seg[None, :])
        & (key_pos[None, :] >= 0)
    )


def score_block(query_view, key_block, allowed):
    scores = (
        jnp.einsum("qkgd,ckd->kgqc", query_view, key_block, preferred_element_type=jnp.float32)
        * score_scale
    )
    return jnp.where(allowed[None, None], scores, -1e30)


def score_grads(probs, grad_view, value_block, delta):
    prob_grad = jnp.einsum(
        "qkgd,ckd->kgqc", grad_view, value_block, preferred_element_type=jnp.float32
    )
    return (probs * (prob_grad - delta[..., None])).astype(jnp.bfloat16)


def key_grads(probs_low, score_grad, query_view, grad_view):
    key_grad = (
        jnp.einsum("kgqc,qkgd->ckd", score_grad, query_view, preferred_element_type=jnp.float32)
        * score_scale
    )
    value_grad = jnp.einsum(
        "kgqc,qkgd->ckd", probs_low, grad_view, preferred_element_type=jnp.float32
    )
    return (key_grad, value_grad)


def per_device(inputs, queries, out_grad, segment_ids, k_weight, v_weight, k_gain):
    tok_rows = inputs.shape[0]
    head_dim = queries.shape[2]
    kv_local = k_weight.shape[1] // head_dim
    group_size = queries.shape[1] // kv_local
    seq_index = lax.axis_index("seq")
    reach_count = WIN // TOK_DEV
    row_base = seq_index * tok_rows
    local_pos = row_base + jnp.arange(tok_rows, dtype=jnp.int32)
    k_full, v_full = (
        lax.all_gather(k_weight, "seq", axis=0, tiled=True),
        lax.all_gather(v_weight, "seq", axis=0, tiled=True),
    )
    k_raw = jnp.dot(inputs, k_full, preferred_element_type=jnp.float32)
    v_raw = jnp.dot(inputs, v_full, preferred_element_type=jnp.float32)
    k_raw = k_raw.reshape(tok_rows, kv_local, head_dim)
    k_inv = lax.rsqrt(jnp.mean(k_raw * k_raw, axis=-1, keepdims=True) + 1e-06)
    k_normed = k_raw * k_inv
    keys_own = (k_normed * k_gain).astype(jnp.bfloat16)
    values_own = v_raw.astype(jnp.bfloat16).reshape(tok_rows, kv_local, head_dim)
    key_list = [keys_own]
    value_list = [values_own]
    seg_list = [segment_ids]
    for offset in range(1, reach_count + 1):
        prior_keys, prior_values, prior_seg = shifted(
            (keys_own, values_own, segment_ids), "seq", offset
        )
        key_list = [prior_keys] + key_list
        value_list = [prior_values] + value_list
        seg_list = [prior_seg] + seg_list
    key_block = jnp.concatenate(key_list, 0)
    value_block = jnp.concatenate(value_list, 0)
    key_seg = jnp.concatenate(seg_list, 0)
    key_pos = (
        row_base
        - reach_count * tok_rows
        + jnp.arange((reach_count + 1) * tok_rows, dtype=jnp.int32)
    )
    query_view = queries.reshape(tok_rows, kv_local, group_size, head_dim)
    grad_view = out_grad.reshape(tok_rows, kv_local, group_size, head_dim)
    allowed = make_allowed(local_pos, segment_ids, key_pos, key_seg)
    scores = score_block(query_view, key_block, allowed)
    row_peak = jnp.max(scores, axis=-1, keepdims=True)
    log_total = row_peak[..., 0] + jnp.log(jnp.sum(jnp.exp(scores - row_peak), axis=-1))
    probs = jnp.exp(scores - log_total[..., None])
    probs_low = probs.astype(jnp.bfloat16)
    attn_out = jnp.einsum(
        "kgqc,ckd->qkgd", probs_low, value_block, preferred_element_type=jnp.float32
    )
    delta = jnp.transpose(jnp.sum(grad_view.astype(jnp.float32) * attn_out, axis=-1), (1, 2, 0))
    score_grad = score_grads(probs, grad_view, value_block, delta)
    query_grad = (
        jnp.einsum("kgqc,ckd->qkgd", score_grad, key_block, preferred_element_type=jnp.float32)
        * score_scale
    )
    key_all, value_all = key_grads(probs_low, score_grad, query_view, grad_view)
    own_lower = reach_count * tok_rows
    key_grad = key_all[own_lower:]
    value_grad = value_all[own_lower:]
    for offset in range(1, reach_count + 1):
        lower = (reach_count - offset) * tok_rows
        back_keys, back_values = shifted(
            (key_all[lower : lower + tok_rows], value_all[lower : lower + tok_rows]), "seq", -offset
        )
        key_grad = key_grad + back_keys
        value_grad = value_grad + back_values
    normed_grad = key_grad * k_gain
    raw_grad = (
        normed_grad - k_normed * jnp.mean(normed_grad * k_normed, axis=-1, keepdims=True)
    ) * k_inv
    raw_low = raw_grad.astype(jnp.bfloat16).reshape(tok_rows, kv_local * head_dim)
    value_low = value_grad.astype(jnp.bfloat16).reshape(tok_rows, kv_local * head_dim)
    input_term = jnp.dot(raw_low, k_full.T, preferred_element_type=jnp.float32)
    input_term = input_term + jnp.dot(value_low, v_full.T, preferred_element_type=jnp.float32)
    inputs_grad = lax.psum_scatter(
        input_term.astype(jnp.bfloat16), "head", scatter_dimension=1, tiled=True
    )
    both_grads = jnp.concatenate([raw_low, value_low], 1)
    split_at = kv_local * head_dim
    weight_rows_grad = lax.psum_scatter(
        lax.dot_general(
            inputs, both_grads, (((0,), (0,)), ((), ())), preferred_element_type=jnp.float32
        ),
        "seq",
        scatter_dimension=0,
        tiled=True,
    )
    return (
        inputs_grad,
        query_grad.astype(jnp.bfloat16).reshape(tok_rows, kv_local * group_size, head_dim),
        weight_rows_grad[:, :split_at],
        weight_rows_grad[:, split_at:],
    )


def solution(mesh):
    in_specs = (
        P("seq", None),
        P("seq", "head", None),
        P("seq", "head", None),
        P("seq"),
        P("seq", "head"),
        P("seq", "head"),
        P(),
    )
    out_specs = (P("seq", "head"), P("seq", "head", None), P("seq", "head"), P("seq", "head"))
    return jax.shard_map(
        per_device, mesh=mesh, in_specs=in_specs, out_specs=out_specs, check_vma=False
    )
```

profile of v0, /device:TPU:1, one launch (start us, length us, event | category | flops | bytes accessed | tf_op | source)
XLA Modules:
  0.0 1416.5 jit_solution(10435968799041910594)
XLA Ops:
  7.2 0.7 all-gather.5.cloned.1.call-update
  7.9 0.7 all-gather.7.cloned.1.call-update
  8.7 4.4 collective-permute-start
  13.1 3.1 collective-permute-start.1
  16.2 2.0 copy.58
  18.3 2.1 copy.79
  20.4 0.7 pad_add_fusion
  21.1 3.2 fusion.6
  24.3 243.2 %all-gather.5.cloned.1.call-done = bf16[64,84,256]{2,1,0:T(8,128)(2,1)} async-done(((bf16[1,84,256]{2,1,0:T(8,128)(2,1)}), bf16[64,84,256]{2,1,0:T(8,128)(2,1)}) %all-gather.5.cloned.1.call-update) | async-done | bytes 2752528 | tf_op jit(solution)/shard_map/all_gather | solution.py:63
  267.5 3.6 reshape.143
  271.1 6.0 multiply_reduce_fusion.1
  277.1 1.2 copy.48
  278.3 0.9 multiply_convert_fusion.1
  279.2 2.0 collective-permute-start.3
  281.2 2.7 collective-permute-start.2
  283.9 284.6 %all-gather.7.cloned.1.call-done = bf16[64,84,256]{2,1,0:T(8,128)(2,1)} async-done(((bf16[1,84,256]{2,1,0:T(8,128)(2,1)}), bf16[64,84,256]{2,1,0:T(8,128)(2,1)}) %all-gather.7.cloned.1.call-update) | async-done | bytes 2752528 | tf_op jit(solution)/shard_map/all_gather | solution.py:64
  568.5 3.6 reshape.145
  572.1 4.9 convolution_convert_fusion
  577.0 1.1 copy.50
  578.1 1.4 collective-permute-start.5
  579.5 2.6 collective-permute-start.4
  582.2 4.2 fusion.3
  586.4 2.8 exponential_reduce_fusion
  589.3 3.7 fusion.11
  593.0 8.2 fusion.1
  601.2 4.8 fusion.8
  606.0 1.3 collective-permute-start.6
  607.3 1.3 collective-permute-start.7
  608.7 6.6 convolution_bitcast_fusion.1
  615.2 1.2 fusion.29
  616.4 1.3 collective-permute-start.8
  617.7 1.5 collective-permute-start.9
  619.3 2.6 collective-permute-done.7
  622.8 4.5 collective-permute-done.8
  627.3 6.8 collective-permute-done.9
  634.1 1.5 fusion.13
  635.6 8.5 convolution_bitcast_fusion
  644.1 3.4 fusion.31
  647.5 4.0 add_convert_fusion
  651.5 0.6 copy-done.10
  652.1 0.6 dynamic-slice
  653.3 4.1 fusion.10
  657.5 1.1 copy.64
  658.5 644.2 %all-reduce.3.cloned.1.call-done = f32[5376,512]{0,1:T(8,128)} async-done(((f32[5376,512]{0,1:T(8,128)}), f32[5376,512]{0,1:T(8,128)}) %all-reduce.3.cloned.1.call-update) | async-done | bytes 11010064
  1302.7 1.2 fusion.28
  1303.9 0.7 copy.66
  1304.6 0.7 copy.65
  1305.3 104.7 %reduce-scatter.3.cloned.1.call-done = bf16[512,1344]{0,1:T(8,128)(2,1)} async-done(((bf16[512,5376]{0,1:T(8,128)(2,1)}), bf16[512,1344]{0,1:T(8,128)(2,1)}) %reduce-scatter.3.cloned.1.call-update) | async-done | bytes 1376272 | tf_op jit(solution)/shard_map/reduce_scatter | solution.py:127
  (44 shorter events, 1.3 us)
Async XLA Ops:
  7.2 260.3 %all-gather.5.cloned.1.call-start = ((), (), s32[]{:S(2)}) async-start(), calls=%async_computation.2 | async-start | bytes 2928640 | tf_op jit(solution)/shard_map/all_gather | solution.py:63
  7.9 560.6 %all-gather.7.cloned.1.call-start = ((), (), s32[]{:S(2)}) async-start(), calls=%async_computation.3 | async-start | bytes 2928640 | tf_op jit(solution)/shard_map/all_gather | solution.py:64
  8.6 1294.0 %all-reduce.3.cloned.1.call-start = ((), (), s32[]{:S(2)}) async-start(), calls=%async_computation.4 | async-start | bytes 22020096
  8.7 11.7 collective-permute-start
  13.1 7.3 collective-permute-start.1
  271.0 7.2 copy-start
  271.1 7.3 copy-start.7
  279.2 302.9 %collective-permute-start.3 = (bf16[512,2,128]{2,0,1:T(8,128)(2,1)}, bf16[512,2,128]{2,0,1:T(8,128)(2,1)}, u32[]{:S(2)}, u32[]{:S(2)}) collective-permute-start(bf16[512,2,128]{2,0,1:T(8,128)(2,1)} %multiply_convert_fusion.1), channel_id=1, source_target_pairs={{0,4},{4,8},{8,12},{12,16},{16,20},{20,24},{24,28},{28,32},{32,36}... | collective-permute-start | bytes 786440 | tf_op jit(solution)/shard_map/ppermute | solution.py:14
  281.2 300.9 %collective-permute-start.2 = (bf16[512,2,128]{2,0,1:T(8,128)(2,1)}, bf16[512,2,128]{2,0,1:T(8,128)(2,1)}, u32[]{:S(2)}, u32[]{:S(2)}) collective-permute-start(bf16[512,2,128]{2,0,1:T(8,128)(2,1)} %multiply_convert_fusion.1), channel_id=1, source_target_pairs={{0,8},{4,12},{8,16},{12,20},{16,24},{20,28},{24,32},{28,36},{32,40... | collective-permute-start | bytes 786440 | tf_op jit(solution)/shard_map/ppermute | solution.py:14
  578.1 8.3 copy-start.2
  578.1 11.1 collective-permute-start.5
  579.5 9.7 collective-permute-start.4
  586.4 6.6 copy-start.1
  586.4 2.8 copy-start.5
  589.2 3.7 copy-start.8
  589.3 3.7 copy-start.9
  601.2 7.5 copy-start.3
  601.2 7.5 copy-start.6
  606.0 13.2 collective-permute-start.6
  607.3 14.5 %collective-permute-start.7 = (f32[512,2,128]{2,0,1:T(8,128)S(1)}, f32[512,2,128]{2,0,1:T(8,128)S(1)}, u32[]{:S(2)}, u32[]{:S(2)}) collective-permute-start(f32[512,2,128]{2,0,1:T(8,128)S(1)} %get-tuple-element.23), channel_id=1, source_target_pairs={{8,0},{12,4},{16,8},{20,12},{24,16},{28,20},{32,24},{36,28},{40,32... | collective-permute-start | bytes 1572872 | tf_op jit(solution)/shard_map/ppermute | solution.py:14
  615.2 7.0 copy-start.4
  616.4 10.9 collective-permute-start.8
  617.7 16.4 %collective-permute-start.9 = (f32[512,2,128]{0,2,1:T(8,128)}, f32[512,2,128]{0,2,1:T(8,128)}, u32[]{:S(2)}, u32[]{:S(2)}) collective-permute-start(f32[512,2,128]{0,2,1:T(8,128)} %get-tuple-element.21), channel_id=1, source_target_pairs={{8,0},{12,4},{16,8},{20,12},{24,16},{28,20},{32,24},{36,28},{40,32... | collective-permute-start | bytes 1572872 | tf_op jit(solution)/shard_map/ppermute | solution.py:14
  644.1 765.9 %reduce-scatter.3.cloned.1.call-start = ((), (), s32[]{:S(2)}) async-start(), calls=%async_computation.1 | async-start | bytes 6881280 | tf_op jit(solution)/shard_map/reduce_scatter | solution.py:127
  651.4 0.7 copy-start.10
Sparse Core Ops, SparseCore 0:
  9.8 257.6 all-gather.4
  269.3 299.1 all-gather.6
  644.2 658.4 all-reduce.2
  1305.9 104.0 reduce-scatter.2
where the time goes:
time: 1420 us
  waiting for transfers between devices  1290 us (91%)
  matrix products  58.2 us (4%)
  starting transfers between devices  21.7 us (2%)
  local copies, waits for them, and re-layouts  20 us (1%)
  between operations  14.8 us (1%)
    unnamed x5, waiting for transfers between devices  646 us
    all_gather x1, waiting for transfers between devices, per_device(): lax.all_gather(v_weight, 'seq', axis=0, tiled=True)  285 us
    all_gather x1, waiting for transfers between devices, per_device(): lax.all_gather(k_weight, 'seq', axis=0, tiled=True)  243 us
    reduce_scatter x1, waiting for transfers between devices, per_device(): lax.psum_scatter(input_term.astype(jnp.bfloat16), 'head', scatter_dimensi...  105 us
  transfers between devices with their start and end apart: 14, of which 7 were waited for; matrix products, arithmetic and copies ran while one was open for 4% of the time, Pallas kernels for 0%

commit v1 on v0

--- a/solution.py
+++ b/solution.py
@@ -61,7 +61,9 @@
     local_pos = row_base + jnp.arange(tok_rows, dtype=jnp.int32)
     k_full, v_full = (
         lax.all_gather(k_weight, "seq", axis=0, tiled=True),
-        lax.all_gather(v_weight, "seq", axis=0, tiled=True),
+        jnp.concatenate(
+            lax.all_to_all(jnp.stack([v_weight] * lax.axis_size("seq")), "seq", 0, 0), axis=0
+        ),
     )
     k_raw = jnp.dot(inputs, k_full, preferred_element_type=jnp.float32)
     v_raw = jnp.dot(inputs, v_full, preferred_element_type=jnp.float32)

time: 1420 us -> 1140 us (0.80)
  waiting for transfers between devices: 1290 us -> 1010 us
    all_gather x1 -> x0, waiting for transfers between devices: 285 us -> none  [per_device(): lax.all_gather(v_weight, 'seq', axis=0, tiled=True)]
    ppermute x10, waiting for transfers between devices: 13.9 us -> 63.3 us  [shifted(): return lax.ppermute(block, axis, route)]
    all_gather x1, waiting for transfers between devices: 243 us -> 194 us  [per_device(): lax.all_gather(k_weight, 'seq', axis=0, tiled=True)]
    unnamed x5 -> x4, waiting for transfers between devices: 646 us -> 644 us
  transfers between devices with their start and end apart: 14 -> 14, of which waited for: 7 -> 7; matrix products, arithmetic and copies ran while one was open for 4% -> 5% of each run, Pallas kernels for 0% -> 0%
where the time goes in v1:
time: 1140 us
  waiting for transfers between devices  1010 us (89%)
  matrix products  58.3 us (5%)
  starting transfers between devices  33.3 us (3%)
  local copies, waits for them, and re-layouts  21 us (2%)
  between operations  14.9 us (1%)
    unnamed x4, waiting for transfers between devices  644 us
    all_gather x1, waiting for transfers between devices, per_device(): lax.all_gather(k_weight, 'seq', axis=0, tiled=True)  194 us
    reduce_scatter x1, waiting for transfers between devices, per_device(): lax.psum_scatter(input_term.astype(jnp.bfloat16), 'head', scatter_dimensi...  105 us
    ppermute x10, waiting for transfers between devices, shifted(): return lax.ppermute(block, axis, route)  63.3 us
  transfers between devices with their start and end apart: 14, of which 7 were waited for; matrix products, arithmetic and copies ran while one was open for 5% of the time, Pallas kernels for 0%

profile of v1, /device:TPU:1, one launch (start us, length us, event | category | flops | bytes accessed | tf_op | source)
XLA Modules:
  0.0 1141.6 jit_solution(6748334286839300832)
XLA Ops:
  7.2 0.7 all-gather.3.cloned.1.call-update
  7.9 2.6 stack.2
  10.5 13.8 %all-to-all-start = ((bf16[64,84,256]{2,1,0:T(8,128)(2,1)}), bf16[64,84,256]{2,1,0:T(8,128)(2,1)}, u32[]{:S(2)}, u32[]{:S(2)}) async-start(bf16[64,84,256]{2,1,0:T(8,128)(2,1)} %stack.2), calls=%async_computation | async-start | bytes 5767168 | tf_op jit(solution)/shard_map/all_to_all | solution.py:65
  24.4 2.9 collective-permute-start
  27.2 3.1 collective-permute-start.1
  30.4 1.5 copy.58
  31.8 1.1 copy.79
  33.0 49.3 %collective-permute-done = s32[512]{0:T(512)S(1)} collective-permute-done((s32[512]{0:T(512)S(1)}, s32[512]{0:T(512)S(1)}, u32[]{:S(2)}, u32[]{:S(2)}) %collective-permute-start) | collective-permute-done | bytes 2080 | tf_op jit(solution)/shard_map/ppermute | solution.py:14
  82.3 2.5 fusion.6
  84.9 194.0 %all-gather.3.cloned.1.call-done = bf16[64,84,256]{2,1,0:T(8,128)(2,1)} async-done(((bf16[1,84,256]{2,1,0:T(8,128)(2,1)}), bf16[64,84,256]{2,1,0:T(8,128)(2,1)}) %all-gather.3.cloned.1.call-update) | async-done | bytes 2752528 | tf_op jit(solution)/shard_map/all_gather | solution.py:63
  278.9 3.6 reshape.149
  282.5 6.0 multiply_reduce_fusion.1
  288.5 1.2 copy.48
  289.8 0.9 multiply_convert_fusion.1
  290.7 2.5 collective-permute-start.3
  293.2 2.0 collective-permute-start.2
  295.2 3.6 reshape.142
  298.7 4.9 convolution_convert_fusion
  303.6 1.1 copy.50
  304.8 2.0 collective-permute-start.5
  306.8 1.5 collective-permute-start.4
  308.3 4.2 fusion.3
  312.6 2.8 exponential_reduce_fusion
  315.4 3.7 fusion.11
  319.1 8.2 fusion.1
  327.4 4.8 fusion.8
  332.2 1.3 collective-permute-start.6
  333.5 1.3 collective-permute-start.7
  334.9 6.6 convolution_bitcast_fusion.1
  341.4 1.2 fusion.29
  342.6 1.3 collective-permute-start.8
  343.9 1.5 collective-permute-start.9
  345.4 2.1 collective-permute-done.7
  348.5 5.0 collective-permute-done.8
  353.5 6.8 collective-permute-done.9
  360.3 1.5 fusion.13
  361.8 8.5 convolution_bitcast_fusion
  370.3 3.4 fusion.31
  373.7 4.0 add_convert_fusion
  377.7 0.6 copy-done.13
  378.4 0.6 dynamic-slice
  379.6 4.1 fusion.10
  383.7 1.1 copy.64
  384.8 642.8 %all-reduce.3.cloned.1.call-done = f32[5376,512]{0,1:T(8,128)} async-done(((f32[5376,512]{0,1:T(8,128)}), f32[5376,512]{0,1:T(8,128)}) %all-reduce.3.cloned.1.call-update) | async-done | bytes 11010064
  1027.6 1.2 fusion.28
  1028.8 0.7 copy.66
  1029.5 0.7 copy.65
  1030.2 104.8 %reduce-scatter.3.cloned.1.call-done = bf16[512,1344]{0,1:T(8,128)(2,1)} async-done(((bf16[512,5376]{0,1:T(8,128)(2,1)}), bf16[512,1344]{0,1:T(8,128)(2,1)}) %reduce-scatter.3.cloned.1.call-update) | async-done | bytes 1376272 | tf_op jit(solution)/shard_map/reduce_scatter | solution.py:129
  (50 shorter events, 1.2 us)
Async XLA Ops:
  7.2 17.2 %copy-start.9 = (s32[512]{0:T(512)S(1)}, s32[512]{0:T(512)}, u32[]{:S(2)}) copy-start(s32[512]{0:T(512)} %param.10) | copy-start | bytes 6148
  7.2 23.2 %copy-start.5 = (bf16[512,4,128]{2,1,0:T(4,128)(2,1)S(1)}, bf16[512,4,128]{2,1,0:T(4,128)(2,1)}, u32[]{:S(2)}) copy-start(bf16[512,4,128]{2,1,0:T(4,128)(2,1)} %param.8) | copy-start | bytes 1572868
  7.2 24.7 %copy-start.6 = (bf16[512,4,128]{2,1,0:T(4,128)(2,1)S(1)}, bf16[512,4,128]{2,1,0:T(4,128)(2,1)}, u32[]{:S(2)}) copy-start(bf16[512,4,128]{2,1,0:T(4,128)(2,1)} %param.9) | copy-start | bytes 1572868
  7.2 271.7 %all-gather.3.cloned.1.call-start = ((), (), s32[]{:S(2)}) async-start(), calls=%async_computation.3 | async-start | bytes 2928640 | tf_op jit(solution)/shard_map/all_gather | solution.py:63
  10.5 284.7 %all-to-all-start = ((bf16[64,84,256]{2,1,0:T(8,128)(2,1)}), bf16[64,84,256]{2,1,0:T(8,128)(2,1)}, u32[]{:S(2)}, u32[]{:S(2)}) async-start(bf16[64,84,256]{2,1,0:T(8,128)(2,1)} %stack.2), calls=%async_computation | async-start | bytes 5767168 | tf_op jit(solution)/shard_map/all_to_all | solution.py:65
  24.3 1003.3 %all-reduce.3.cloned.1.call-start = ((), (), s32[]{:S(2)}) async-start(), calls=%async_computation.4 | async-start | bytes 22020096
  24.4 58.0 %collective-permute-start = (s32[512]{0:T(512)S(1)}, s32[512]{0:T(512)S(1)}, u32[]{:S(2)}, u32[]{:S(2)}) collective-permute-start(s32[512]{0:T(512)S(1)} %copy-done.9), channel_id=1, source_target_pairs={{0,8},{4,12},{8,16},{12,20},{16,24},{20,28},{24,32},{28,36},{32,40... | collective-permute-start | bytes 6152 | tf_op jit(solution)/shard_map/ppermute | solution.py:14
  27.2 55.1 %collective-permute-start.1 = (s32[512]{0:T(512)S(1)}, s32[512]{0:T(512)S(1)}, u32[]{:S(2)}, u32[]{:S(2)}) collective-permute-start(s32[512]{0:T(512)S(1)} %copy-done.9), channel_id=1, source_target_pairs={{0,4},{4,8},{8,12},{12,16},{16,20},{20,24},{24,28},{28,32},{32,36}... | collective-permute-start | bytes 6152 | tf_op jit(solution)/shard_map/ppermute | solution.py:14
  282.5 7.2 copy-start
  282.5 7.3 copy-start.10
  290.7 17.7 %collective-permute-start.3 = (bf16[512,2,128]{2,0,1:T(8,128)(2,1)}, bf16[512,2,128]{2,0,1:T(8,128)(2,1)}, u32[]{:S(2)}, u32[]{:S(2)}) collective-permute-start(bf16[512,2,128]{2,0,1:T(8,128)(2,1)} %multiply_convert_fusion.1), channel_id=1, source_target_pairs={{0,4},{4,8},{8,12},{12,16},{16,20},{20,24},{24,28},{28,32},{32,36}... | collective-permute-start | bytes 786440 | tf_op jit(solution)/shard_map/ppermute | solution.py:14
  293.2 15.2 %collective-permute-start.2 = (bf16[512,2,128]{2,0,1:T(8,128)(2,1)}, bf16[512,2,128]{2,0,1:T(8,128)(2,1)}, u32[]{:S(2)}, u32[]{:S(2)}) collective-permute-start(bf16[512,2,128]{2,0,1:T(8,128)(2,1)} %multiply_convert_fusion.1), channel_id=1, source_target_pairs={{0,8},{4,12},{8,16},{12,20},{16,24},{20,28},{24,32},{28,36},{32,40... | collective-permute-start | bytes 786440 | tf_op jit(solution)/shard_map/ppermute | solution.py:14
  304.8 7.8 copy-start.2
  304.8 10.6 collective-permute-start.5
  306.8 8.6 collective-permute-start.4
  312.6 6.6 copy-start.1
  312.6 2.8 copy-start.7
  315.4 3.7 copy-start.11
  315.4 3.7 copy-start.12
  327.4 7.5 copy-start.3
  327.4 7.5 copy-start.8
  332.2 13.2 %collective-permute-start.6 = (f32[512,2,128]{2,0,1:T(8,128)S(1)}, f32[512,2,128]{2,0,1:T(8,128)S(1)}, u32[]{:S(2)}, u32[]{:S(2)}) collective-permute-start(f32[512,2,128]{2,0,1:T(8,128)S(1)} %get-tuple-element.22), channel_id=1, source_target_pairs={{4,0},{8,4},{12,8},{16,12},{20,16},{24,20},{28,24},{32,28},{36,32}... | collective-permute-start | bytes 1572872 | tf_op jit(solution)/shard_map/ppermute | solution.py:14
  333.5 14.0 %collective-permute-start.7 = (f32[512,2,128]{2,0,1:T(8,128)S(1)}, f32[512,2,128]{2,0,1:T(8,128)S(1)}, u32[]{:S(2)}, u32[]{:S(2)}) collective-permute-start(f32[512,2,128]{2,0,1:T(8,128)S(1)} %get-tuple-element.23), channel_id=1, source_target_pairs={{8,0},{12,4},{16,8},{20,12},{24,16},{28,20},{32,24},{36,28},{40,32... | collective-permute-start | bytes 1572872 | tf_op jit(solution)/shard_map/ppermute | solution.py:14
  341.4 6.5 copy-start.4
  342.6 10.9 collective-permute-start.8
  343.9 16.4 %collective-permute-start.9 = (f32[512,2,128]{0,2,1:T(8,128)}, f32[512,2,128]{0,2,1:T(8,128)}, u32[]{:S(2)}, u32[]{:S(2)}) collective-permute-start(f32[512,2,128]{0,2,1:T(8,128)} %get-tuple-element.21), channel_id=1, source_target_pairs={{8,0},{12,4},{16,8},{20,12},{24,16},{28,20},{32,24},{36,28},{40,32... | collective-permute-start | bytes 1572872 | tf_op jit(solution)/shard_map/ppermute | solution.py:14
  370.3 764.8 %reduce-scatter.3.cloned.1.call-start = ((), (), s32[]{:S(2)}) async-start(), calls=%async_computation.2 | async-start | bytes 6881280 | tf_op jit(solution)/shard_map/reduce_scatter | solution.py:129
  377.7 0.7 copy-start.13
Sparse Core Ops, SparseCore 0:
  9.8 269.0 all-gather.2
  370.4 657.1 all-reduce.2
  1031.0 104.0 reduce-scatter.2
